TPU v7x, 32 devices: a whole 2x2x4 slice. The times are simulated.
32 devices in a mesh: tx: 8 (over z, x), ty: 4 (over y, core).
Axes of the slice: x: 2, y: 2, z: 4, core: 2. Of those that a mesh axis runs over, the one named last changes fastest.
Arguments:
- dynamics_residual: float32 [6, 48, 48, 16], P(None, 'tx', 'ty'), may hold values from -6 to 6
- density: float32 [6, 48, 48, 16], P(None, 'tx', 'ty'), may hold values from 0.5 to 8
- diagonal_gain: float32 [6, 48, 48, 16], P(None, 'tx', 'ty'), may hold values from 0.05 to 2
- vertical_coupling: float32 [6, 48, 48, 16], P(None, 'tx', 'ty'), may hold values from 0.2 to 8
- edge_panel: int32 [6, 4], replicated, may hold values from 0 to 5, as said below
- edge_side: int32 [6, 4], replicated, may hold values from 0 to 3, as said below
- edge_flip: int32 [6, 4], replicated, may hold values from 0 to 1, as said below
Outputs:
- solution: float32 [6, 48, 48, 16], P(None, 'tx', 'ty')
- coarse_correction: float32 [6, 24, 24, 16], P(None, 'tx', 'ty')
Inputs may be any that keep to these rules, and one draw needn't show every extreme that they name: The six panels are the faces of a cube, each with its own orientation and label: side s of panel p borders side edge_side[p, s] of panel edge_panel[p, s], the pairing is mutual, and no side borders a side of its own panel. `edge_side`: see edge_panel. `edge_flip`: equal on both sides of a bordering pair.
All inputs are finite; a program needn't handle non-finite values.
Results may differ from a plain program's by a relative error of at most 0.00005.
Values sent between devices are 32-bit elements; how exact they have to be, the bound alone decides.
A program may use at most 64 MiB of HBM per device.

v0:
```python
import jax
import jax.numpy as jnp
from jax import lax
from jax.sharding import PartitionSpec as P

relaxation = 0.8
highest = lax.Precision.HIGHEST


def extended(x, sides, width):
    for axis, dim in sides:
        count, length = (lax.axis_size(axis), x.shape[dim])
        up = [(i, (i + 1) % count) for i in range(count - 1)]
        down = [(j, i) for i, j in up]
        last = lax.slice_in_dim(x, length - width, length, axis=dim)
        first = lax.slice_in_dim(x, 0, width, axis=dim)
        before = lax.ppermute(last, axis, up)
        after = lax.ppermute(first, axis, down)
        x = jnp.concatenate([before, x, after], axis=dim)
    return x


def partner(value, axis, distance):
    mask = 2**distance
    pairs = [(source, source ^ mask) for source in range(lax.axis_size(axis))]
    return lax.ppermute(value, axis, pairs)


def lower_levels(values):
    return jnp.concatenate([jnp.zeros_like(values[..., :1]), values[..., :-1]], axis=-1)


def upper_levels(values):
    return jnp.concatenate([values[..., 1:], jnp.zeros_like(values[..., :1])], axis=-1)


def vertical_part(grid_field, vertical):
    return vertical * (grid_field - upper_levels(grid_field)) + lower_levels(vertical) * (
        grid_field - lower_levels(grid_field)
    )


def diagonal_of(cell_gain, vertical, horizontal):
    return cell_gain + 4.0 * horizontal + vertical + lower_levels(vertical)


def neighbour_sum(padded):
    return padded[:, :-2, 1:-1] + padded[:, 2:, 1:-1] + padded[:, 1:-1, :-2] + padded[:, 1:-1, 2:]


def apply_operator(grid_field, padded, cell_gain, vertical, horizontal):
    return (
        cell_gain * grid_field
        + horizontal * (4.0 * grid_field - neighbour_sum(padded))
        + vertical_part(grid_field, vertical)
    )


def restrict(values):
    shaped = values.reshape(
        values.shape[0], values.shape[1] // 2, 2, values.shape[2] // 2, 2, values.shape[3]
    )
    return shaped.mean(axis=(2, 4))


def prolong(values):
    return jnp.repeat(jnp.repeat(values, 2, axis=1), 2, axis=2)


def window_piece(held_block, positions, offset):
    length = held_block.shape[2]
    local_index = positions - offset
    inside = ((local_index >= 0) & (local_index < length)).astype(jnp.float32)
    picked = jnp.take(held_block, jnp.clip(local_index, 0, length - 1), axis=2)
    return picked * inside[None, None, :, None]


def select_rims(forward, mirrored, edge_panel, edge_side, edge_flip, first_side):
    side_codes = edge_side[:, first_side : first_side + 2]
    panel_codes = edge_panel[:, first_side : first_side + 2]
    flip_codes = edge_flip[:, first_side : first_side + 2].astype(jnp.float32)
    matched = (
        (side_codes[:, :, None, None] == jnp.arange(4)[None, None, :, None])
        & (panel_codes[:, :, None, None] == jnp.arange(6)[None, None, None, :])
    ).astype(jnp.float32)
    straight = matched * (1.0 - flip_codes)[:, :, None, None]
    turned = matched * flip_codes[:, :, None, None]
    return jnp.einsum("pstq,tqjl->psjl", straight, forward, precision=highest) + jnp.einsum(
        "pstq,tqjl->psjl", turned, mirrored, precision=highest
    )


def padded_tile(grid_field, edge_panel, edge_side, edge_flip):
    row_index = lax.axis_index("tx")
    col_index = lax.axis_index("ty")
    row_count = lax.axis_size("tx")
    col_count = lax.axis_size("ty")
    tile_rows = grid_field.shape[1]
    tile_cols = grid_field.shape[2]
    side_cells = tile_rows * row_count
    padded = extended(grid_field, (("tx", 1), ("ty", 2)), 1)
    across_mask = jnp.stack([row_index == 0, row_index == row_count - 1]).astype(jnp.float32)
    along_mask = jnp.stack([col_index == 0, col_index == col_count - 1]).astype(jnp.float32)
    row_sides = jnp.stack([grid_field[:, 0], grid_field[:, -1]]) * across_mask[:, None, None, None]
    col_sides = (
        jnp.stack([grid_field[:, :, 0], grid_field[:, :, -1]]) * along_mask[:, None, None, None]
    )
    col_block = lax.psum(row_sides, "tx")
    row_block = lax.psum(col_sides, "ty")
    col_positions = col_index * tile_cols + jnp.arange(tile_cols)
    row_positions = row_index * tile_rows + jnp.arange(tile_rows)
    cross_cols = jnp.stack(
        [
            window_piece(row_block, col_positions, row_index * tile_rows),
            window_piece(row_block, side_cells - 1 - col_positions, row_index * tile_rows),
        ]
    )
    summed_cols = lax.psum(cross_cols, "tx")
    cross_rows = jnp.stack(
        [
            window_piece(col_block, row_positions, col_index * tile_cols),
            window_piece(col_block, side_cells - 1 - row_positions, col_index * tile_cols),
        ]
    )
    summed_rows = lax.psum(cross_rows, "ty")
    mirror_rowblock = row_block[:, :, ::-1]
    for bit in range(row_count.bit_length() - 1):
        mirror_rowblock = partner(mirror_rowblock, "tx", bit)
    mirror_colblock = col_block[:, :, ::-1]
    for bit in range(col_count.bit_length() - 1):
        mirror_colblock = partner(mirror_colblock, "ty", bit)
    cols_forward = jnp.concatenate([col_block, summed_cols[0]], axis=0)
    cols_mirror = jnp.concatenate([mirror_colblock, summed_cols[1]], axis=0)
    rows_forward = jnp.concatenate([summed_rows[0], row_block], axis=0)
    rows_mirror = jnp.concatenate([summed_rows[1], mirror_rowblock], axis=0)
    col_rims = select_rims(cols_forward, cols_mirror, edge_panel, edge_side, edge_flip, 0)
    row_rims = select_rims(rows_forward, rows_mirror, edge_panel, edge_side, edge_flip, 2)
    top_rim = jnp.where(row_index == 0, col_rims[:, 0], padded[:, 0, 1:-1])
    bottom_rim = jnp.where(row_index == row_count - 1, col_rims[:, 1], padded[:, -1, 1:-1])
    left_rim = jnp.where(col_index == 0, row_rims[:, 0], padded[:, 1:-1, 0])
    right_rim = jnp.where(col_index == col_count - 1, row_rims[:, 1], padded[:, 1:-1, -1])
    padded = padded.at[:, 0, 1:-1].set(top_rim)
    padded = padded.at[:, -1, 1:-1].set(bottom_rim)
    padded = padded.at[:, 1:-1, 0].set(left_rim)
    padded = padded.at[:, 1:-1, -1].set(right_rim)
    return padded


def shards(
    dynamics_residual, density, diagonal_gain, vertical_coupling, edge_panel, edge_side, edge_flip
):
    right_side = density * dynamics_residual
    fine_diagonal = diagonal_of(diagonal_gain, vertical_coupling, 1.0)
    smoothed = relaxation * right_side / fine_diagonal
    applied = apply_operator(
        smoothed,
        padded_tile(smoothed, edge_panel, edge_side, edge_flip),
        diagonal_gain,
        vertical_coupling,
        1.0,
    )
    coarse_rhs = restrict(right_side - applied)
    coarse_gain = restrict(diagonal_gain)
    coarse_vertical = restrict(vertical_coupling)
    coarse_diagonal = diagonal_of(coarse_gain, coarse_vertical, 0.25)
    coarse_guess = relaxation * coarse_rhs / coarse_diagonal
    coarse_applied = apply_operator(
        coarse_guess,
        padded_tile(coarse_guess, edge_panel, edge_side, edge_flip),
        coarse_gain,
        coarse_vertical,
        0.25,
    )
    coarse_correction = coarse_guess + relaxation * (coarse_rhs - coarse_applied) / coarse_diagonal
    corrected = smoothed + prolong(coarse_correction)
    final_applied = apply_operator(
        corrected,
        padded_tile(corrected, edge_panel, edge_side, edge_flip),
        diagonal_gain,
        vertical_coupling,
        1.0,
    )
    solution = corrected + relaxation * (right_side - final_applied) / fine_diagonal
    return (solution, coarse_correction)


def solution(mesh):
    placed = (
        P(None, "tx", "ty", None),
        P(None, "tx", "ty", None),
        P(None, "tx", "ty", None),
        P(None, "tx", "ty", None),
        P(),
        P(),
        P(),
    )
    return jax.shard_map(
        shards,
        mesh=mesh,
        in_specs=placed,
        out_specs=(P(None, "tx", "ty", None), P(None, "tx", "ty", None)),
        check_vma=False,
    )
```

profile of v0, /device:TPU:0, one launch (start us, length us, event | category | flops | bytes accessed | tf_op | source)
XLA Modules:
  0.0 281.6 jit_solution(7349908816677631455)
XLA Ops:
  0.7 1.2 copy.130
  1.8 1.6 fusion.17
  3.6 13.3 %psum.85 = f32[2,6,6,16]{3,1,0,2:T(8,128)S(1)} all-reduce(f32[2,6,6,16]{3,1,0,2:T(8,128)S(1)} %maximum_multiply_fusion.2), channel_id=1, replica_groups=mesh['tx'=8,'ty'=4] {'ty'}, use_global_device_ids=true, to_apply=%region_1.0 | all-reduce | flops 1152 | bytes 9216 | tf_op jit(solution)/shard_map/psum | solution.py:109
  16.9 1.6 collective-permute-start.6
  18.5 1.3 collective-permute-start.1
  19.8 4.5 %collective-permute-start = (f32[6,1,12,16]{3,0,2,1:T(8,128)S(1)}, f32[6,1,12,16]{3,0,2,1:T(8,128)S(1)}, u32[]{:S(2)}, u32[]{:S(2)}) collective-permute-start(f32[6,1,12,16]{3,0,2,1:T(8,128)S(1)} %get-tuple-element.193), channel_id=1, source_target_pairs={{0,4},{4,8},{8,12},{12,16},{16,20},{20,24},{24,28},{1,5},{5,9},{9,... | collective-permute-start | bytes 13832 | tf_op jit(solution)/shard_map/ppermute | solution.py:17
  25.9 38.7 %all-reduce.10 = (f32[2,2,6,12,16]{4,2,1,3,0:T(8,128)S(1)}, f32[2,6,12,16]{3,1,0,2:T(8,128)S(1)}) all-reduce(f32[2,2,6,12,16]{4,2,1,3,0:T(8,128)S(1)} %pad_maximum_fusion.2, f32[2,6,12,16]{3,1,0,2:T(8,128)S(1)} %copy.51), channel_id=1, replica_groups=mesh['tx'=8,'ty'=4] {'tx'}, use_global_device_ids=true, to_apply=%region_2.4 | all-reduce | flops 6912 | bytes 55296 | tf_op jit(solution)/shard_map/psum | solution.py:118
  64.9 0.7 copy-done.16
  69.0 11.5 %psum.87 = f32[2,2,6,6,16]{4,2,1,3,0:T(8,128)S(1)} all-reduce(f32[2,2,6,6,16]{4,2,1,3,0:T(8,128)S(1)} %pad_maximum_fusion.5), channel_id=1, replica_groups=mesh['tx'=8,'ty'=4] {'ty'}, use_global_device_ids=true, to_apply=%region_3.6 | all-reduce | flops 2304 | bytes 18432 | tf_op jit(solution)/shard_map/psum | solution.py:125
  81.6 2.0 collective-permute-start.2
  83.6 1.3 collective-permute-start.3
  85.3 3.7 %collective-permute-done.7 = f32[2,6,6,16]{3,1,0,2:T(8,128)S(1)} collective-permute-done((f32[2,6,6,16]{3,1,0,2:T(8,128)S(1)}, f32[2,6,6,16]{3,1,0,2:T(8,128)S(1)}, u32[]{:S(2)}, u32[]{:S(2)}) %collective-permute-start.7) | collective-permute-done | bytes 4640 | tf_op jit(solution)/shard_map/ppermute | solution.py:26
  89.2 4.0 %collective-permute-start.5 = (f32[2,6,12,16]{3,1,0,2:T(8,128)S(1)}, f32[2,6,12,16]{3,1,0,2:T(8,128)S(1)}, u32[]{:S(2)}, u32[]{:S(2)}) collective-permute-start(f32[2,6,12,16]{3,1,0,2:T(8,128)S(1)} %collective-permute-done.4), channel_id=1, source_target_pairs={{0,2},{1,3},{2,0},{3,1},{4,6},{5,7},{6,4},{7,5},{8,10},{9,11},{10,... | collective-permute-start | bytes 27656 | tf_op jit(solution)/shard_map/ppermute | solution.py:26
  93.1 2.0 collective-permute-done.8
  96.4 1.3 fusion.58
  97.7 0.7 fusion.16
  98.8 10.7 %psum.89 = f32[2,6,3,16]{3,1,0,2:T(8,128)S(1)} all-reduce(f32[2,6,3,16]{3,1,0,2:T(8,128)S(1)} %maximum_multiply_fusion.4), channel_id=1, replica_groups=mesh['tx'=8,'ty'=4] {'ty'}, use_global_device_ids=true, to_apply=%region_8.11 | all-reduce | flops 576 | bytes 4608 | tf_op jit(solution)/shard_map/psum | solution.py:109
  111.0 37.9 %all-reduce.9 = (f32[2,2,6,6,16]{4,2,1,3,0:T(8,128)S(1)}, f32[2,6,6,16]{3,1,0,2:T(8,128)S(1)}) all-reduce(f32[2,2,6,6,16]{4,2,1,3,0:T(8,128)S(1)} %pad_maximum_fusion.6, f32[2,6,6,16]{3,1,0,2:T(8,128)S(1)} %copy.60), channel_id=1, replica_groups=mesh['tx'=8,'ty'=4] {'tx'}, use_global_device_ids=true, to_apply=%region_9.13 | all-reduce | flops 3456 | bytes 27648 | tf_op jit(solution)/shard_map/psum | solution.py:118
  150.3 10.5 %psum.91 = f32[2,2,6,3,16]{4,2,1,3,0:T(8,128)S(1)} all-reduce(f32[2,2,6,3,16]{4,2,1,3,0:T(8,128)S(1)} %pad_maximum_fusion.8), channel_id=1, replica_groups=mesh['tx'=8,'ty'=4] {'ty'}, use_global_device_ids=true, to_apply=%region_10.15 | all-reduce | flops 1152 | bytes 9216 | tf_op jit(solution)/shard_map/psum | solution.py:125
  160.8 1.3 collective-permute-start.10
  162.1 4.5 %collective-permute-start.9 = (f32[6,1,6,16]{3,0,2,1:T(8,128)S(1)}, f32[6,1,6,16]{3,0,2,1:T(8,128)S(1)}, u32[]{:S(2)}, u32[]{:S(2)}) collective-permute-start(f32[6,1,6,16]{3,0,2,1:T(8,128)S(1)} %get-tuple-element.213), channel_id=1, source_target_pairs={{0,4},{4,8},{8,12},{12,16},{16,20},{20,24},{24,28},{1,5},{5,9},{9,... | collective-permute-start | bytes 6920 | tf_op jit(solution)/shard_map/ppermute | solution.py:17
  167.0 1.1 collective-permute-done.9
  168.2 1.3 collective-permute-start.11
  169.4 1.3 collective-permute-start.12
  170.8 1.8 collective-permute-start.16
  173.0 3.2 %collective-permute-start.13 = (f32[2,6,6,16]{3,1,0,2:T(8,128)S(1)}, f32[2,6,6,16]{3,1,0,2:T(8,128)S(1)}, u32[]{:S(2)}, u32[]{:S(2)}) collective-permute-start(f32[2,6,6,16]{3,1,0,2:T(8,128)S(1)} %rev.20), channel_id=1, source_target_pairs={{0,1},{1,0},{2,3},{3,2},{4,5},{5,4},{6,7},{7,6},{8,9},{9,8},{10,11... | collective-permute-start | bytes 13832 | tf_op jit(solution)/shard_map/ppermute | solution.py:26
  177.1 2.9 %collective-permute-start.14 = (f32[2,6,6,16]{3,1,0,2:T(8,128)S(1)}, f32[2,6,6,16]{3,1,0,2:T(8,128)S(1)}, u32[]{:S(2)}, u32[]{:S(2)}) collective-permute-start(f32[2,6,6,16]{3,1,0,2:T(8,128)S(1)} %collective-permute-done.13), channel_id=1, source_target_pairs={{0,2},{1,3},{2,0},{3,1},{4,6},{5,7},{6,4},{7,5},{8,10},{9,11},{10,... | collective-permute-start | bytes 13832 | tf_op jit(solution)/shard_map/ppermute | solution.py:26
  180.0 1.2 collective-permute-done.17
  182.6 1.3 fusion.90
  184.2 11.0 %psum.93 = f32[2,6,6,16]{3,1,0,2:T(8,128)S(1)} all-reduce(f32[2,6,6,16]{3,1,0,2:T(8,128)S(1)} %copy_multiply_fusion.3), channel_id=1, replica_groups=mesh['tx'=8,'ty'=4] {'ty'}, use_global_device_ids=true, to_apply=%region_12.17 | all-reduce | flops 1152 | bytes 9216 | tf_op jit(solution)/shard_map/psum | solution.py:109
  196.9 0.6 slice_bitcast_fusion.35
  197.9 39.3 %all-reduce.8 = (f32[2,2,6,12,16]{4,2,1,3,0:T(8,128)S(1)}, f32[2,6,12,16]{3,1,0,2:T(8,128)S(1)}) all-reduce(f32[2,2,6,12,16]{4,2,1,3,0:T(8,128)S(1)} %pad_maximum_fusion.3, f32[2,6,12,16]{3,1,0,2:T(8,128)S(1)} %copy.67), channel_id=1, replica_groups=mesh['tx'=8,'ty'=4] {'tx'}, use_global_device_ids=true, to_apply=%region_13.18 | all-reduce | flops 6912 | bytes 55296 | tf_op jit(solution)/shard_map/psum | solution.py:118
  238.8 11.1 %psum.95 = f32[2,2,6,6,16]{4,2,1,3,0:T(8,128)S(1)} all-reduce(f32[2,2,6,6,16]{4,2,1,3,0:T(8,128)S(1)} %pad_maximum_fusion.7), channel_id=1, replica_groups=mesh['tx'=8,'ty'=4] {'ty'}, use_global_device_ids=true, to_apply=%region_14.19 | all-reduce | flops 2304 | bytes 18432 | tf_op jit(solution)/shard_map/psum | solution.py:125
  249.9 0.8 copy-done.5
  250.7 1.3 collective-permute-start.19
  252.0 4.7 %collective-permute-start.18 = (f32[6,1,12,16]{3,0,2,1:T(8,128)S(1)}, f32[6,1,12,16]{3,0,2,1:T(8,128)S(1)}, u32[]{:S(2)}, u32[]{:S(2)}) collective-permute-start(f32[6,1,12,16]{3,0,2,1:T(8,128)S(1)} %copy-done.4), channel_id=1, source_target_pairs={{0,4},{4,8},{8,12},{12,16},{16,20},{20,24},{24,28},{1,5},{5,9},{9,... | collective-permute-start | bytes 13832 | tf_op jit(solution)/shard_map/ppermute | solution.py:17
  257.3 1.1 collective-permute-done.18
  258.5 1.6 collective-permute-start.20
  260.1 1.3 collective-permute-start.21
  261.4 4.4 %collective-permute-start.25 = (f32[2,6,6,16]{3,1,0,2:T(8,128)}, f32[2,6,6,16]{3,1,0,2:T(8,128)}, u32[]{:S(2)}, u32[]{:S(2)}) collective-permute-start(f32[2,6,6,16]{3,1,0,2:T(8,128)} %collective-permute-done.24), channel_id=1, source_target_pairs={{0,8},{4,12},{8,0},{12,4},{16,24},{20,28},{24,16},{28,20},{1,9},{5... | collective-permute-start | bytes 13832 | tf_op jit(solution)/shard_map/ppermute | solution.py:26
  266.3 0.6 copy.74
  267.6 3.3 %collective-permute-start.22 = (f32[2,6,12,16]{3,1,0,2:T(8,128)}, f32[2,6,12,16]{3,1,0,2:T(8,128)S(1)}, u32[]{:S(2)}, u32[]{:S(2)}) collective-permute-start(f32[2,6,12,16]{3,1,0,2:T(8,128)} %rev.22), channel_id=1, source_target_pairs={{0,1},{1,0},{2,3},{3,2},{4,5},{5,4},{6,7},{7,6},{8,9},{9,8},{10,11... | collective-permute-start | bytes 27656 | tf_op jit(solution)/shard_map/ppermute | solution.py:26
  271.0 1.0 collective-permute-done.22
  272.0 2.3 collective-permute-start.23
  274.3 2.6 collective-permute-done.26
  278.7 1.3 fusion.54
  280.0 0.8 fusion.12
  280.8 0.8 copy.73
  (191 shorter events, 21.4 us)
Async XLA Ops:
  0.6 1.2 copy-start
  0.6 1.2 copy-start.1
  16.9 68.0 %collective-permute-start.6 = (f32[2,6,6,16]{3,1,0,2:T(8,128)S(1)}, f32[2,6,6,16]{3,1,0,2:T(8,128)S(1)}, u32[]{:S(2)}, u32[]{:S(2)}) collective-permute-start(f32[2,6,6,16]{3,1,0,2:T(8,128)S(1)} %rev.19), channel_id=1, source_target_pairs={{0,4},{4,0},{8,12},{12,8},{16,20},{20,16},{24,28},{28,24},{1,5},{5... | collective-permute-start | bytes 13832 | tf_op jit(solution)/shard_map/ppermute | solution.py:26
  18.5 63.1 %collective-permute-start.1 = (f32[6,1,12,16]{3,0,2,1:T(8,128)S(1)}, f32[6,1,12,16]{3,0,2,1:T(8,128)S(1)}, u32[]{:S(2)}, u32[]{:S(2)}) collective-permute-start(f32[6,1,12,16]{3,0,2,1:T(8,128)S(1)} %get-tuple-element.192), channel_id=1, source_target_pairs={{4,0},{8,4},{12,8},{16,12},{20,16},{24,20},{28,24},{5,1},{9,5},{13... | collective-permute-start | bytes 13832 | tf_op jit(solution)/shard_map/ppermute | solution.py:18
  19.8 61.8 %collective-permute-start = (f32[6,1,12,16]{3,0,2,1:T(8,128)S(1)}, f32[6,1,12,16]{3,0,2,1:T(8,128)S(1)}, u32[]{:S(2)}, u32[]{:S(2)}) collective-permute-start(f32[6,1,12,16]{3,0,2,1:T(8,128)S(1)} %get-tuple-element.193), channel_id=1, source_target_pairs={{0,4},{4,8},{8,12},{12,16},{16,20},{20,24},{24,28},{1,5},{5,9},{9,... | collective-permute-start | bytes 13832 | tf_op jit(solution)/shard_map/ppermute | solution.py:17
  64.7 24.5 %collective-permute-start.4 = (f32[2,6,12,16]{3,1,0,2:T(8,128)S(1)}, f32[2,6,12,16]{3,1,0,2:T(8,128)S(1)}, u32[]{:S(2)}, u32[]{:S(2)}) collective-permute-start(f32[2,6,12,16]{3,1,0,2:T(8,128)S(1)} %rev.18), channel_id=1, source_target_pairs={{0,1},{1,0},{2,3},{3,2},{4,5},{5,4},{6,7},{7,6},{8,9},{9,8},{10,11... | collective-permute-start | bytes 27656 | tf_op jit(solution)/shard_map/ppermute | solution.py:26
  64.8 0.7 copy-start.16
  65.5 115.7 %copy-start.14 = (f32[6,2]{0,1:T(2,128)}, f32[6,2]{0,1:T(2,128)S(1)}, u32[]{:S(2)}) copy-start(f32[6,2]{0,1:T(2,128)S(1)} %get-tuple-element.218) | copy-start | bytes 148
  65.5 116.6 %copy-start.9 = (f32[6,2]{0,1:T(2,128)}, f32[6,2]{0,1:T(2,128)S(1)}, u32[]{:S(2)}) copy-start(f32[6,2]{0,1:T(2,128)S(1)} %get-tuple-element.219) | copy-start | bytes 148
  65.6 101.1 %copy-start.19 = (f32[6,2]{0,1:T(2,128)}, f32[6,2]{0,1:T(2,128)S(1)}, u32[]{:S(2)}) copy-start(f32[6,2]{0,1:T(2,128)S(1)} %get-tuple-element.224) | copy-start | bytes 148
  65.8 0.7 copy-start.17
  66.6 114.6 %copy-start.6 = (pred[6,2,6]{2,0,1:T(8,128)(4,1)}, pred[6,2,6]{2,0,1:T(8,128)(4,1)S(1)}, u32[]{:S(2)}) copy-start(pred[6,2,6]{2,0,1:T(8,128)(4,1)S(1)} %iota_compare_fusion) | copy-start | bytes 220
  66.6 0.7 copy-start.18
  67.3 113.9 %copy-start.11 = (pred[6,2,4]{0,2,1:T(4,128)(4,1)}, pred[6,2,4]{0,2,1:T(4,128)(4,1)S(1)}, u32[]{:S(2)}) copy-start(pred[6,2,4]{0,2,1:T(4,128)(4,1)S(1)} %iota_compare_fusion.2) | copy-start | bytes 148
  81.6 7.5 %collective-permute-start.2 = (f32[6,8,1,16]{3,0,1,2:T(8,128)S(1)}, f32[6,8,1,16]{3,0,1,2:T(8,128)S(1)}, u32[]{:S(2)}, u32[]{:S(2)}) collective-permute-start(f32[6,8,1,16]{3,0,1,2:T(8,128)S(1)} %get-tuple-element.178), channel_id=1, source_target_pairs={{0,1},{1,2},{2,3},{4,5},{5,6},{6,7},{8,9},{9,10},{10,11},{12,13},{... | collective-permute-start | bytes 9224 | tf_op jit(solution)/shard_map/ppermute | solution.py:17
  83.6 5.5 %collective-permute-start.3 = (f32[6,8,1,16]{3,0,1,2:T(8,128)S(1)}, f32[6,8,1,16]{3,0,1,2:T(8,128)S(1)}, u32[]{:S(2)}, u32[]{:S(2)}) collective-permute-start(f32[6,8,1,16]{3,0,1,2:T(8,128)S(1)} %get-tuple-element.179), channel_id=1, source_target_pairs={{1,0},{2,1},{3,2},{5,4},{6,5},{7,6},{9,8},{10,9},{11,10},{13,12},{... | collective-permute-start | bytes 9224 | tf_op jit(solution)/shard_map/ppermute | solution.py:18
  84.9 4.2 %collective-permute-start.7 = (f32[2,6,6,16]{3,1,0,2:T(8,128)S(1)}, f32[2,6,6,16]{3,1,0,2:T(8,128)S(1)}, u32[]{:S(2)}, u32[]{:S(2)}) collective-permute-start(f32[2,6,6,16]{3,1,0,2:T(8,128)S(1)} %collective-permute-done.6), channel_id=1, source_target_pairs={{0,8},{4,12},{8,0},{12,4},{16,24},{20,28},{24,16},{28,20},{1,9},{5... | collective-permute-start | bytes 13832 | tf_op jit(solution)/shard_map/ppermute | solution.py:26
  89.1 6.0 %collective-permute-start.8 = (f32[2,6,6,16]{3,1,0,2:T(8,128)S(1)}, f32[2,6,6,16]{3,1,0,2:T(8,128)S(1)}, u32[]{:S(2)}, u32[]{:S(2)}) collective-permute-start(f32[2,6,6,16]{3,1,0,2:T(8,128)S(1)} %collective-permute-done.7), channel_id=1, source_target_pairs={{0,16},{4,20},{8,24},{12,28},{16,0},{20,4},{24,8},{28,12},{1,17},{... | collective-permute-start | bytes 13832 | tf_op jit(solution)/shard_map/ppermute | solution.py:26
  89.2 6.6 %collective-permute-start.5 = (f32[2,6,12,16]{3,1,0,2:T(8,128)S(1)}, f32[2,6,12,16]{3,1,0,2:T(8,128)S(1)}, u32[]{:S(2)}, u32[]{:S(2)}) collective-permute-start(f32[2,6,12,16]{3,1,0,2:T(8,128)S(1)} %collective-permute-done.4), channel_id=1, source_target_pairs={{0,2},{1,3},{2,0},{3,1},{4,6},{5,7},{6,4},{7,5},{8,10},{9,11},{10,... | collective-permute-start | bytes 27656 | tf_op jit(solution)/shard_map/ppermute | solution.py:26
  95.7 2.0 copy-start.3
  96.4 1.4 copy-start.2
  109.5 61.2 %collective-permute-start.15 = (f32[2,6,3,16]{3,1,0,2:T(8,128)S(1)}, f32[2,6,3,16]{3,1,0,2:T(8,128)S(1)}, u32[]{:S(2)}, u32[]{:S(2)}) collective-permute-start(f32[2,6,3,16]{3,1,0,2:T(8,128)S(1)} %rev.21), channel_id=1, source_target_pairs={{0,4},{4,0},{8,12},{12,8},{16,20},{20,16},{24,28},{28,24},{1,5},{5... | collective-permute-start | bytes 6920 | tf_op jit(solution)/shard_map/ppermute | solution.py:26
  160.8 6.3 %collective-permute-start.10 = (f32[6,1,6,16]{3,0,1,2:T(8,128)S(1)}, f32[6,1,6,16]{3,0,1,2:T(8,128)S(1)}, u32[]{:S(2)}, u32[]{:S(2)}) collective-permute-start(f32[6,1,6,16]{3,0,1,2:T(8,128)S(1)} %get-tuple-element.212), channel_id=1, source_target_pairs={{4,0},{8,4},{12,8},{16,12},{20,16},{24,20},{28,24},{5,1},{9,5},{13... | collective-permute-start | bytes 6920 | tf_op jit(solution)/shard_map/ppermute | solution.py:18
  162.1 6.1 %collective-permute-start.9 = (f32[6,1,6,16]{3,0,2,1:T(8,128)S(1)}, f32[6,1,6,16]{3,0,2,1:T(8,128)S(1)}, u32[]{:S(2)}, u32[]{:S(2)}) collective-permute-start(f32[6,1,6,16]{3,0,2,1:T(8,128)S(1)} %get-tuple-element.213), channel_id=1, source_target_pairs={{0,4},{4,8},{8,12},{12,16},{16,20},{20,24},{24,28},{1,5},{5,9},{9,... | collective-permute-start | bytes 6920 | tf_op jit(solution)/shard_map/ppermute | solution.py:17
  168.2 8.6 %collective-permute-start.11 = (f32[6,5,1,16]{3,0,1,2:T(8,128)S(1)}, f32[6,5,1,16]{3,0,1,2:T(8,128)S(1)}, u32[]{:S(2)}, u32[]{:S(2)}) collective-permute-start(f32[6,5,1,16]{3,0,1,2:T(8,128)S(1)} %get-tuple-element.200), channel_id=1, source_target_pairs={{0,1},{1,2},{2,3},{4,5},{5,6},{6,7},{8,9},{9,10},{10,11},{12,13},{... | collective-permute-start | bytes 5768 | tf_op jit(solution)/shard_map/ppermute | solution.py:17
  169.4 7.3 %collective-permute-start.12 = (f32[6,5,1,16]{3,0,1,2:T(8,128)S(1)}, f32[6,5,1,16]{3,0,1,2:T(8,128)S(1)}, u32[]{:S(2)}, u32[]{:S(2)}) collective-permute-start(f32[6,5,1,16]{3,0,1,2:T(8,128)S(1)} %get-tuple-element.201), channel_id=1, source_target_pairs={{1,0},{2,1},{3,2},{5,4},{6,5},{7,6},{9,8},{10,9},{11,10},{13,12},{... | collective-permute-start | bytes 5768 | tf_op jit(solution)/shard_map/ppermute | solution.py:18
  170.8 5.5 %collective-permute-start.16 = (f32[2,6,3,16]{3,1,0,2:T(8,128)S(1)}, f32[2,6,3,16]{3,1,0,2:T(8,128)S(1)}, u32[]{:S(2)}, u32[]{:S(2)}) collective-permute-start(f32[2,6,3,16]{3,1,0,2:T(8,128)S(1)} %collective-permute-done.15), channel_id=1, source_target_pairs={{0,8},{4,12},{8,0},{12,4},{16,24},{20,28},{24,16},{28,20},{1,9},{5... | collective-permute-start | bytes 6920 | tf_op jit(solution)/shard_map/ppermute | solution.py:26
  173.0 4.1 %collective-permute-start.13 = (f32[2,6,6,16]{3,1,0,2:T(8,128)S(1)}, f32[2,6,6,16]{3,1,0,2:T(8,128)S(1)}, u32[]{:S(2)}, u32[]{:S(2)}) collective-permute-start(f32[2,6,6,16]{3,1,0,2:T(8,128)S(1)} %rev.20), channel_id=1, source_target_pairs={{0,1},{1,0},{2,3},{3,2},{4,5},{5,4},{6,7},{7,6},{8,9},{9,8},{10,11... | collective-permute-start | bytes 13832 | tf_op jit(solution)/shard_map/ppermute | solution.py:26
  176.3 5.0 %collective-permute-start.17 = (f32[2,6,3,16]{3,1,0,2:T(8,128)S(1)}, f32[2,6,3,16]{3,1,0,2:T(8,128)S(1)}, u32[]{:S(2)}, u32[]{:S(2)}) collective-permute-start(f32[2,6,3,16]{3,1,0,2:T(8,128)S(1)} %collective-permute-done.16), channel_id=1, source_target_pairs={{0,16},{4,20},{8,24},{12,28},{16,0},{20,4},{24,8},{28,12},{1,17},{... | collective-permute-start | bytes 6920 | tf_op jit(solution)/shard_map/ppermute | solution.py:26
  177.1 5.0 %collective-permute-start.14 = (f32[2,6,6,16]{3,1,0,2:T(8,128)S(1)}, f32[2,6,6,16]{3,1,0,2:T(8,128)S(1)}, u32[]{:S(2)}, u32[]{:S(2)}) collective-permute-start(f32[2,6,6,16]{3,1,0,2:T(8,128)S(1)} %collective-permute-done.13), channel_id=1, source_target_pairs={{0,2},{1,3},{2,0},{3,1},{4,6},{5,7},{6,4},{7,5},{8,10},{9,11},{10,... | collective-permute-start | bytes 13832 | tf_op jit(solution)/shard_map/ppermute | solution.py:26
  238.5 22.9 %collective-permute-start.24 = (f32[2,6,6,16]{3,1,0,2:T(8,128)}, f32[2,6,6,16]{3,1,0,2:T(8,128)}, u32[]{:S(2)}, u32[]{:S(2)}) collective-permute-start(f32[2,6,6,16]{3,1,0,2:T(8,128)} %rev.23), channel_id=1, source_target_pairs={{0,4},{4,0},{8,12},{12,8},{16,20},{20,16},{24,28},{28,24},{1,5},{5... | collective-permute-start | bytes 13832 | tf_op jit(solution)/shard_map/ppermute | solution.py:26
  249.9 0.8 copy-start.5
  249.9 2.1 copy-start.4
  250.7 6.7 %collective-permute-start.19 = (f32[6,1,12,16]{3,0,1,2:T(8,128)S(1)}, f32[6,1,12,16]{3,0,1,2:T(8,128)S(1)}, u32[]{:S(2)}, u32[]{:S(2)}) collective-permute-start(f32[6,1,12,16]{3,0,1,2:T(8,128)S(1)} %copy-done.5), channel_id=1, source_target_pairs={{4,0},{8,4},{12,8},{16,12},{20,16},{24,20},{28,24},{5,1},{9,5},{13... | collective-permute-start | bytes 13832 | tf_op jit(solution)/shard_map/ppermute | solution.py:18
  252.0 6.5 %collective-permute-start.18 = (f32[6,1,12,16]{3,0,2,1:T(8,128)S(1)}, f32[6,1,12,16]{3,0,2,1:T(8,128)S(1)}, u32[]{:S(2)}, u32[]{:S(2)}) collective-permute-start(f32[6,1,12,16]{3,0,2,1:T(8,128)S(1)} %copy-done.4), channel_id=1, source_target_pairs={{0,4},{4,8},{8,12},{12,16},{16,20},{20,24},{24,28},{1,5},{5,9},{9,... | collective-permute-start | bytes 13832 | tf_op jit(solution)/shard_map/ppermute | solution.py:17
  258.5 7.4 %copy-start.20 = (f32[6,2]{0,1:T(2,128)S(1)}, f32[6,2]{0,1:T(2,128)}, u32[]{:S(2)}) copy-start(f32[6,2]{0,1:T(2,128)} %copy-done.19) | copy-start | bytes 148
  258.5 7.4 %copy-start.7 = (pred[6,2,6]{2,0,1:T(8,128)(4,1)S(1)}, pred[6,2,6]{2,0,1:T(8,128)(4,1)}, u32[]{:S(2)}) copy-start(pred[6,2,6]{2,0,1:T(8,128)(4,1)} %copy-done.6) | copy-start | bytes 220
  258.5 12.4 %collective-permute-start.20 = (f32[6,8,1,16]{3,0,1,2:T(8,128)S(1)}, f32[6,8,1,16]{3,0,1,2:T(8,128)S(1)}, u32[]{:S(2)}, u32[]{:S(2)}) collective-permute-start(f32[6,8,1,16]{3,0,1,2:T(8,128)S(1)} %get-tuple-element.176), channel_id=1, source_target_pairs={{0,1},{1,2},{2,3},{4,5},{5,6},{6,7},{8,9},{9,10},{10,11},{12,13},{... | collective-permute-start | bytes 9224 | tf_op jit(solution)/shard_map/ppermute | solution.py:17
  260.1 5.7 %copy-start.12 = (pred[6,2,4]{0,2,1:T(4,128)(4,1)S(1)}, pred[6,2,4]{0,2,1:T(4,128)(4,1)}, u32[]{:S(2)}) copy-start(pred[6,2,4]{0,2,1:T(4,128)(4,1)} %copy-done.11) | copy-start | bytes 148
  260.1 10.8 %collective-permute-start.21 = (f32[6,8,1,16]{3,0,1,2:T(8,128)S(1)}, f32[6,8,1,16]{3,0,1,2:T(8,128)S(1)}, u32[]{:S(2)}, u32[]{:S(2)}) collective-permute-start(f32[6,8,1,16]{3,0,1,2:T(8,128)S(1)} %get-tuple-element.177), channel_id=1, source_target_pairs={{1,0},{2,1},{3,2},{5,4},{6,5},{7,6},{9,8},{10,9},{11,10},{13,12},{... | collective-permute-start | bytes 9224 | tf_op jit(solution)/shard_map/ppermute | solution.py:18
  261.4 9.5 %collective-permute-start.25 = (f32[2,6,6,16]{3,1,0,2:T(8,128)}, f32[2,6,6,16]{3,1,0,2:T(8,128)}, u32[]{:S(2)}, u32[]{:S(2)}) collective-permute-start(f32[2,6,6,16]{3,1,0,2:T(8,128)} %collective-permute-done.24), channel_id=1, source_target_pairs={{0,8},{4,12},{8,0},{12,4},{16,24},{20,28},{24,16},{28,20},{1,9},{5... | collective-permute-start | bytes 13832 | tf_op jit(solution)/shard_map/ppermute | solution.py:26
  267.6 4.5 %collective-permute-start.22 = (f32[2,6,12,16]{3,1,0,2:T(8,128)}, f32[2,6,12,16]{3,1,0,2:T(8,128)S(1)}, u32[]{:S(2)}, u32[]{:S(2)}) collective-permute-start(f32[2,6,12,16]{3,1,0,2:T(8,128)} %rev.22), channel_id=1, source_target_pairs={{0,1},{1,0},{2,3},{3,2},{4,5},{5,4},{6,7},{7,6},{8,9},{9,8},{10,11... | collective-permute-start | bytes 27656 | tf_op jit(solution)/shard_map/ppermute | solution.py:26
  270.9 6.0 %collective-permute-start.26 = (f32[2,6,6,16]{3,1,0,2:T(8,128)}, f32[2,6,6,16]{3,1,0,2:T(8,128)S(1)}, u32[]{:S(2)}, u32[]{:S(2)}) collective-permute-start(f32[2,6,6,16]{3,1,0,2:T(8,128)} %collective-permute-done.25), channel_id=1, source_target_pairs={{0,16},{4,20},{8,24},{12,28},{16,0},{20,4},{24,8},{28,12},{1,17},{... | collective-permute-start | bytes 13832 | tf_op jit(solution)/shard_map/ppermute | solution.py:26
  270.9 6.0 %copy-start.8 = (pred[6,2,6]{2,0,1:T(8,128)(4,1)S(1)}, pred[6,2,6]{2,0,1:T(8,128)(4,1)}, u32[]{:S(2)}) copy-start(pred[6,2,6]{2,0,1:T(8,128)(4,1)} %copy-done.6) | copy-start | bytes 220
  270.9 6.0 %copy-start.15 = (f32[6,2]{0,1:T(2,128)S(1)}, f32[6,2]{0,1:T(2,128)}, u32[]{:S(2)}) copy-start(f32[6,2]{0,1:T(2,128)} %copy-done.14) | copy-start | bytes 148
  271.0 5.9 %copy-start.13 = (pred[6,2,4]{0,2,1:T(4,128)(4,1)S(1)}, pred[6,2,4]{0,2,1:T(4,128)(4,1)}, u32[]{:S(2)}) copy-start(pred[6,2,4]{0,2,1:T(4,128)(4,1)} %copy-done.11) | copy-start | bytes 148
  272.0 5.4 %collective-permute-start.23 = (f32[2,6,12,16]{3,1,0,2:T(8,128)S(1)}, f32[2,6,12,16]{3,1,0,2:T(8,128)S(1)}, u32[]{:S(2)}, u32[]{:S(2)}) collective-permute-start(f32[2,6,12,16]{3,1,0,2:T(8,128)S(1)} %collective-permute-done.22), channel_id=1, source_target_pairs={{0,2},{1,3},{2,0},{3,1},{4,6},{5,7},{6,4},{7,5},{8,10},{9,11},{10,... | collective-permute-start | bytes 27656 | tf_op jit(solution)/shard_map/ppermute | solution.py:26
  277.4 0.7 copy-start.10
where the time goes:
time: 282 us
  blocking collectives  184 us (65%)
  starting transfers between devices  50.7 us (18%)
  local copies, waits for them, and re-layouts  15.3 us (5%)
  waiting for transfers between devices  13.8 us (5%)
  other arithmetic  9.88 us (4%)
  matrix products  5.9 us (2%)
    psum x3, blocking collectives, padded_tile(): summed_cols = lax.psum(cross_cols, 'tx')  116 us
    psum x3, blocking collectives, padded_tile(): row_block = lax.psum(col_sides, 'ty')  35 us
    psum x3, blocking collectives, padded_tile(): summed_rows = lax.psum(cross_rows, 'ty')  33.1 us
    ppermute x15, starting transfers between devices, partner(): return lax.ppermute(value, axis, pairs)  24.2 us
    ppermute x6, starting transfers between devices, extended(): before = lax.ppermute(last, axis, up)  18.7 us
    ppermute x15, waiting for transfers between devices, partner(): return lax.ppermute(value, axis, pairs)  11.6 us
    ppermute x6, starting transfers between devices, extended(): after = lax.ppermute(first, axis, down)  7.74 us
    gather x12, local copies, waits for them, and re-layouts, window_piece(): picked = jnp.take(held_block, jnp.clip(local_index, 0, length - 1), axis=2)  6.65 us
  transfers between devices with their start and end apart: 27, of which 10 were waited for; matrix products, arithmetic and copies ran while one was open for 5% of the time, Pallas kernels for 0%

commit v1 on v0

v1 whole, which is shorter than its diff:
```python
import functools

import jax
import jax.numpy as jnp
from jax import lax
from jax.experimental import pallas as pl
from jax.experimental.pallas import tpu as pltpu
from jax.sharding import PartitionSpec as P

MESH = pl.DeviceIdType.MESH
relaxation = 0.8
LANES = 128


def round_up(value, unit):
    return (value + unit - 1) // unit * unit


def kernel(
    nr,
    nc,
    res_hbm,
    den_hbm,
    gain_hbm,
    vert_hbm,
    panel_ref,
    side_ref,
    flip_ref,
    sol_ref,
    corr_ref,
    inp,
    packed,
    spread,
    st_row,
    st_col,
    nb_row,
    nb_col,
    rx_row,
    rx_col,
    in_sem,
    send_sem,
    nb_sem,
    row_sem,
    col_sem,
):
    panels, rows, cols, levels = sol_ref.shape
    half_r, half_c = rows // 2, cols // 2
    k = cols // rows
    height = spread.shape[1] // 2
    r = lax.axis_index("tx")
    c = lax.axis_index("ty")
    is_row = (r == 0) | (r == nr - 1)
    is_col = (c == 0) | (c == nc - 1)
    tr = r // (nr - 1)
    tc = c // (nc - 1)

    def messages(n):
        found = []
        found.append((r > 0, (r - 1, c), st_row.at[n, 0], nb_row.at[n, 1], nb_sem.at[n, 1]))
        found.append((r < nr - 1, (r + 1, c), st_row.at[n, 1], nb_row.at[n, 0], nb_sem.at[n, 0]))
        found.append((c > 0, (r, c - 1), st_col.at[n, 0], nb_col.at[n, 1], nb_sem.at[n, 3]))
        found.append((c < nc - 1, (r, c + 1), st_col.at[n, 1], nb_col.at[n, 0], nb_sem.at[n, 2]))
        for i in range(k):
            src = st_row.at[n, tr, i]
            for f in range(2):
                slot = 4 * f + tr
                i_dst = i if f == 0 else k - 1 - i
                c_dst = c if f == 0 else nc - 1 - c
                r_dst = k * c + i if f == 0 else nr - 1 - k * c - i
                for e in range(2):
                    found.append(
                        (
                            is_row,
                            (e * (nr - 1), c_dst),
                            src,
                            rx_row.at[n, slot, i_dst],
                            row_sem.at[n, slot, i_dst],
                        )
                    )
                    found.append(
                        (
                            is_row,
                            (r_dst, e * (nc - 1)),
                            src,
                            rx_col.at[n, slot],
                            col_sem.at[n, slot],
                        )
                    )
        src = st_col.at[n, tc]
        for f in range(2):
            slot = 4 * f + 2 + tc
            g = r if f == 0 else nr - 1 - r
            for e in range(2):
                found.append(
                    (
                        is_col,
                        (e * (nr - 1), g // k),
                        src,
                        rx_row.at[n, slot, g % k],
                        row_sem.at[n, slot, g % k],
                    )
                )
                found.append(
                    (is_col, (g, e * (nc - 1)), src, rx_col.at[n, slot], col_sem.at[n, slot])
                )
        return found

    def same(dest):
        return (dest[0] == r) & (dest[1] == c)

    barrier = pltpu.get_barrier_semaphore()
    expected = jnp.int32(0)
    for active, dest, _, _, _ in messages(0):
        go = active & jnp.logical_not(same(dest))
        expected = expected + go.astype(jnp.int32)

        @pl.when(go)
        def _():
            pl.semaphore_signal(barrier, inc=1, device_id=dest, device_id_type=MESH)

    loads = [
        pltpu.make_async_copy(source, inp.at[i], in_sem.at[i])
        for i, source in enumerate((den_hbm, res_hbm, gain_hbm, vert_hbm))
    ]
    for load in loads:
        load.start()

    lane = lax.broadcasted_iota(jnp.int32, (height, LANES), 1)
    sub = lax.broadcasted_iota(jnp.int32, (height, LANES), 0)
    level = lane % levels
    first_level = level == 0
    last_level = level == levels - 1

    def lower(x):
        return jnp.where(first_level, 0.0, pltpu.roll(x, 1, 1))

    def upper(x):
        return jnp.where(last_level, 0.0, pltpu.roll(x, LANES - 1, 1))

    seg_h = st_col.shape[2]
    seg_lane = lax.broadcasted_iota(jnp.int32, (seg_h, LANES), 1)

    def pick_tables(side):
        index = seg_lane
        code = jnp.zeros_like(seg_lane)
        for p in range(panels):
            here = seg_lane // levels == p
            index = jnp.where(here, panel_ref[p, side] * levels + seg_lane % levels, index)
            code = jnp.where(here, flip_ref[p, side] * 4 + side_ref[p, side], code)
        return index, code

    row_pick = pick_tables(tr)
    col_pick = pick_tables(2 + tc)

    for load in loads:
        load.wait()

    def pack(value):
        filler = jnp.zeros((rows, cols, LANES - panels * levels), jnp.float32)
        return jnp.concatenate([value[p] for p in range(panels)] + [filler], axis=-1)

    def split(which, value):
        packed[which, :, :cols, :] = value
        if packed.shape[2] > cols:
            packed[which, :, cols:, :] = jnp.zeros(
                (rows, packed.shape[2] - cols, LANES), jnp.float32
            )
        return [
            [packed[which, y, pl.ds(b, height, stride=2), :] for b in range(2)]
            for y in range(rows)
        ]

    every = [(y, b) for y in range(rows) for b in range(2)]

    def fine(fun):
        return [[fun(y, b) for b in range(2)] for y in range(rows)]

    right_side = split(0, pack(inp[0] * inp[1]))
    gain = split(1, pack(inp[2]))
    vertical = split(2, pack(inp[3]))
    low_vert = fine(lambda y, b: lower(vertical[y][b]))
    inverse = fine(
        lambda y, b: relaxation / (gain[y][b] + 4.0 + vertical[y][b] + low_vert[y][b])
    )
    smoothed = fine(lambda y, b: inverse[y][b] * right_side[y][b])

    def start(n):
        for m, (active, dest, src, dst, sem) in enumerate(messages(n)):
            mine = same(dest)

            @pl.when(active & jnp.logical_not(mine))
            def _():
                pltpu.make_async_remote_copy(
                    src_ref=src,
                    dst_ref=dst,
                    send_sem=send_sem.at[n, m],
                    recv_sem=sem,
                    device_id=dest,
                    device_id_type=MESH,
                ).start()

            if m >= 4:

                @pl.when(active & mine)
                def _():
                    pltpu.make_async_copy(src, dst, sem).start()

    def finish_sends(n):
        for m, (active, dest, src, dst, sem) in enumerate(messages(n)):

            @pl.when(active & jnp.logical_not(same(dest)))
            def _():
                pltpu.make_async_copy(src, src, send_sem.at[n, m]).wait()

    def mirrored(x, length):
        lines = [x[length - 1 - s : length - s] for s in range(length)]
        if seg_h > length:
            lines.append(jnp.zeros((seg_h - length, LANES), jnp.float32))
        return jnp.concatenate(lines, axis=0)

    def select(read, pick, length):
        index, code = pick
        parts = []
        for f in range(2):
            taken = jnp.zeros((seg_h, LANES), jnp.float32)
            for t in range(4):
                moved = jnp.take_along_axis(
                    read(4 * f + t), index, axis=1, mode="promise_in_bounds"
                )
                taken = jnp.where(code == 4 * f + t, moved, taken)
            parts.append(taken)
        return jnp.where(code >= 4, mirrored(parts[1], length), parts[0])

    def receive(n, length):
        def arrived(ref, sem):
            pltpu.make_async_copy(ref, ref, sem).wait()

        @pl.when(r > 0)
        def _():
            arrived(nb_row.at[n, 0], nb_sem.at[n, 0])

        @pl.when(r < nr - 1)
        def _():
            arrived(nb_row.at[n, 1], nb_sem.at[n, 1])

        @pl.when(c > 0)
        def _():
            arrived(nb_col.at[n, 0], nb_sem.at[n, 2])

        @pl.when(c < nc - 1)
        def _():
            arrived(nb_col.at[n, 1], nb_sem.at[n, 3])

        @pl.when(is_row)
        def _():
            for slot in range(8):
                for i in range(k):
                    arrived(rx_row.at[n, slot, i], row_sem.at[n, slot, i])
            for i in range(k):
                nb_row[n, tr, i] = select(lambda s: rx_row[n, s, i], row_pick, length)

        @pl.when(is_col)
        def _():
            for slot in range(8):
                arrived(rx_col.at[n, slot], col_sem.at[n, slot])
            nb_col[n, tc] = select(lambda s: rx_col[n, s], col_pick, length)

    def gathered(n, end, b):
        lines = [nb_row[n, end, i, b * half_r : (b + 1) * half_r, :] for i in range(k)]
        if height > half_c:
            lines.append(jnp.zeros((height - half_c, LANES), jnp.float32))
        return jnp.concatenate(lines, axis=0)

    def from_left(x, line):
        return jnp.where(sub == 0, line, pltpu.roll(x, 1, 0))

    def from_right(x, line):
        return jnp.where(sub == half_c - 1, line, pltpu.roll(x, height - 1, 0))

    for end, y in ((0, 0), (1, rows - 1)):
        for i in range(k):
            for b in range(2):
                st_row[0, end, i, b * half_r : (b + 1) * half_r, :] = smoothed[y][b][
                    i * half_r : (i + 1) * half_r
                ]
    for y in range(rows):
        at = (y % 2) * half_r + y // 2
        st_col[0, 0, at : at + 1, :] = smoothed[y][0][0:1]
        st_col[0, 1, at : at + 1, :] = smoothed[y][1][half_c - 1 : half_c]
    pl.semaphore_wait(barrier, expected)
    start(0)

    def inner(y, b):
        x = smoothed[y][b]
        total = vertical[y][b] * upper(x) + low_vert[y][b] * lower(x) + smoothed[y][1 - b]
        if y > 0:
            total = total + smoothed[y - 1][b]
        if y < rows - 1:
            total = total + smoothed[y + 1][b]
        return total

    partial = fine(inner)

    def block_mean(values, i):
        y = 2 * i
        return 0.25 * (values[y][0] + values[y][1] + values[y + 1][0] + values[y + 1][1])

    small = range(half_r)
    c_vert = [block_mean(vertical, i) for i in small]
    c_low = [lower(c_vert[i]) for i in small]
    c_inv = [relaxation / (block_mean(gain, i) + 1.0 + c_vert[i] + c_low[i]) for i in small]

    receive(0, rows)

    def outer(y, b):
        at = (y % 2) * half_r + y // 2
        if b == 0:
            total = partial[y][b] + from_left(smoothed[y][1], nb_col[0, 0, at : at + 1, :])
        else:
            total = partial[y][b] + from_right(smoothed[y][0], nb_col[0, 1, at : at + 1, :])
        if y == 0:
            total = total + gathered(0, 0, b)
        if y == rows - 1:
            total = total + gathered(0, 1, b)
        return total

    off = fine(outer)
    residual = fine(lambda y, b: (1.0 - relaxation) * right_side[y][b] + off[y][b])
    guess = [c_inv[i] * block_mean(residual, i) for i in small]

    def stage_coarse(n, values):
        for end, i in ((0, 0), (1, half_r - 1)):
            for piece in range(k):
                st_row[n, end, piece, :half_r, :] = values[i][
                    piece * half_r : (piece + 1) * half_r
                ]
        for i in small:
            st_col[n, 0, i : i + 1, :] = values[i][0:1]
            st_col[n, 1, i : i + 1, :] = values[i][half_c - 1 : half_c]

    stage_coarse(1, guess)
    start(1)
    c_partial = []
    for i in small:
        x = guess[i]
        beside = jnp.zeros_like(x)
        if i > 0:
            beside = beside + guess[i - 1]
        if i < half_r - 1:
            beside = beside + guess[i + 1]
        c_partial.append(
            (beside, c_vert[i] * upper(x) + c_low[i] * lower(x))
        )
    receive(1, half_r)
    correction = []
    for i in small:
        beside, column = c_partial[i]
        beside = beside + from_left(guess[i], nb_col[1, 0, i : i + 1, :])
        beside = beside + from_right(guess[i], nb_col[1, 1, i : i + 1, :])
        if i == 0:
            beside = beside + gathered(1, 0, 0)
        if i == half_r - 1:
            beside = beside + gathered(1, 1, 0)
        correction.append(
            (2.0 - relaxation) * guess[i] + c_inv[i] * (0.25 * beside + column)
        )

    stage_coarse(2, correction)
    start(2)
    c_up = [upper(x) for x in correction]
    c_down = [lower(x) for x in correction]

    def base(y, b):
        i = y // 2
        total = off[y][b] + 2.0 * correction[i]
        total = total + vertical[y][b] * c_up[i] + low_vert[y][b] * c_down[i]
        other = i - 1 if y % 2 == 0 else i + 1
        if 0 <= other < half_r:
            total = total + correction[other]
        return (
            (2.0 - relaxation) * smoothed[y][b] + (1.0 - relaxation) * correction[i],
            total,
        )

    bases = fine(base)
    for i in small:
        for p in range(panels):
            corr_ref[p, i] = correction[i][:half_c, p * levels : (p + 1) * levels]
    receive(2, half_r)
    left = [from_left(correction[i], nb_col[2, 0, i : i + 1, :]) for i in small]
    right = [from_right(correction[i], nb_col[2, 1, i : i + 1, :]) for i in small]
    top = gathered(2, 0, 0)
    bottom = gathered(2, 1, 0)
    for y, b in every:
        first, total = bases[y][b]
        total = total + (left if b == 0 else right)[y // 2]
        if y == 0:
            total = total + top
        if y == rows - 1:
            total = total + bottom
        spread[y, pl.ds(b, height, stride=2), :] = first + inverse[y][b] * total
    for p in range(panels):
        sol_ref[p] = spread[:, :cols, p * levels : (p + 1) * levels]
    for n in range(3):
        finish_sends(n)


def solution(mesh):
    nr, nc = mesh.shape["tx"], mesh.shape["ty"]

    def shards(residual, density, gain, vertical, edge_panel, edge_side, edge_flip):
        panels, rows, cols, levels = residual.shape
        k = cols // rows
        assert cols == k * rows and rows % 2 == 0 and panels * levels <= LANES
        seg_h = round_up(rows, 8)
        height = round_up(cols // 2, 8)
        tall = 2 * height
        f32 = jnp.float32
        return pl.pallas_call(
            functools.partial(kernel, nr, nc),
            out_shape=(
                jax.ShapeDtypeStruct(residual.shape, f32),
                jax.ShapeDtypeStruct((panels, rows // 2, cols // 2, levels), f32),
            ),
            in_specs=[pl.BlockSpec(memory_space=pl.ANY)] * 4
            + [pl.BlockSpec(memory_space=pltpu.SMEM)] * 3,
            out_specs=(pl.BlockSpec(memory_space=pltpu.VMEM),) * 2,
            scratch_shapes=[
                pltpu.VMEM((4, panels, rows, cols, levels), f32),
                pltpu.VMEM((3, rows, tall, LANES), f32),
                pltpu.VMEM((rows, tall, LANES), f32),
                pltpu.VMEM((3, 2, k, seg_h, LANES), f32),
                pltpu.VMEM((3, 2, seg_h, LANES), f32),
                pltpu.VMEM((3, 2, k, seg_h, LANES), f32),
                pltpu.VMEM((3, 2, seg_h, LANES), f32),
                pltpu.VMEM((3, 8, k, seg_h, LANES), f32),
                pltpu.VMEM((3, 8, seg_h, LANES), f32),
                pltpu.SemaphoreType.DMA((4,)),
                pltpu.SemaphoreType.DMA((3, 4 + 8 * k + 4 + 4)),
                pltpu.SemaphoreType.DMA((3, 4)),
                pltpu.SemaphoreType.DMA((3, 8, k)),
                pltpu.SemaphoreType.DMA((3, 8)),
            ],
            compiler_params=pltpu.CompilerParams(collective_id=0, has_side_effects=True),
        )(residual, density, gain, vertical, edge_panel, edge_side, edge_flip)

    fields = P(None, "tx", "ty", None)
    return jax.shard_map(
        shards,
        mesh=mesh,
        in_specs=(fields,) * 4 + (P(),) * 3,
        out_specs=(fields, fields),
        check_vma=False,
    )
```

time: 282 us -> 29.4 us (0.10)
  blocking collectives: 184 us -> 0 us
  starting transfers between devices: 50.7 us -> 0 us
  Pallas kernels: 0 us -> 23.4 us
  waiting for transfers between devices: 13.8 us -> 0 us
  local copies, waits for them, and re-layouts: 15.3 us -> 5.09 us
  other arithmetic: 9.88 us -> 0 us
  matrix products: 5.9 us -> 0 us
    psum x9 -> x0, blocking collectives: 184 us -> none  [the longest x3 116 us: padded_tile(): summed_cols = lax.psum(cross_cols, 'tx')]
    ppermute x27 -> x0, starting transfers between devices: 50.7 us -> none  [the longest x15 24.2 us: partner(): return lax.ppermute(value, axis, pairs)]
    pallas_call x0 -> x1, Pallas kernels: none -> 23.4 us  [shards(): pl.pallas_call(functools.partial(kernel, nr, nc), out_shape=(jax.ShapeDty...]
    ppermute x27 -> x0, waiting for transfers between devices: 13.8 us -> none  [the longest x15 11.6 us: partner(): return lax.ppermute(value, axis, pairs)]
    gather x12 -> x0, local copies, waits for them, and re-layouts: 6.65 us -> none  [window_piece(): picked = jnp.take(held_block, jnp.clip(local_index, 0, length - 1), axis=2)]
    dot_general x12 -> x0, matrix products: 5.9 us -> none  [the longest x6 2.95 us: select_rims(): jnp.einsum('pstq,tqjl->psjl', turned, mirrored, precision=highest)]
    scatter x12 -> x0, other arithmetic: 3.89 us -> none  [the longest x3 3.81 us: padded_tile(): padded = padded.at[:, 0, 1:-1].set(top_rim)]
  transfers between devices with their start and end apart: 27 -> 0, of which waited for: 10 -> 0; matrix products, arithmetic and copies ran while one was open for 5% -> 0% of each run, Pallas kernels for 0% -> 0%
where the time goes in v1:
time: 29.4 us; the launch traced here: 29.2 us
  Pallas kernels  23.4 us (80%)
  local copies, waits for them, and re-layouts  5.09 us (17%)
  between operations  0.66 us (2%)
    pallas_call x1, Pallas kernels, shards(): pl.pallas_call(functools.partial(kernel, nr, nc), out_shape=(jax.ShapeDty...  23.4 us
    unnamed x11, local copies, waits for them, and re-layouts  5.09 us

profile of v1, /device:TPU:0, one launch (start us, length us, event | category | flops | bytes accessed | tf_op | source)
XLA Modules:
  0.0 29.2 jit_solution(12975660155412439409)
XLA Ops:
  0.6 0.0 copy-start.1
  0.6 1.4 %copy.9.panel_ref = s32[6,4]{1,0:T(8,128)} copy(s32[6,4]{0,1:T(4,128)} %param.11) | data formatting | bytes 192 | tf_op args[4]
  2.0 0.0 copy-done.1
  2.0 0.0 copy-start.2
  2.0 0.7 %copy.10.side_ref = s32[6,4]{1,0:T(8,128)} copy(s32[6,4]{0,1:T(4,128)S(1)} %copy-done.1) | data formatting | bytes 192 | tf_op args[5]
  2.7 0.0 copy-done.2
  2.7 0.7 %copy.11.flip_ref = s32[6,4]{1,0:T(8,128)} copy(s32[6,4]{0,1:T(4,128)S(1)} %copy-done.2) | data formatting | bytes 192 | tf_op args[6]
  3.4 23.4 %shard_map.86 = (f32[6,6,12,16]{3,2,1,0:T(8,128)}, f32[6,3,6,16]{3,2,1,0:T(8,128)}) custom-call(f32[6,6,12,16]{3,2,1,0:T(8,128)} %res_hbm.1, f32[6,6,12,16]{3,2,1,0:T(8,128)} %den_hbm.1, f32[6,6,12,16]{3,2,1,0:T(8,128)} %gain_hbm.1, f32[6,6,12,16]{3,2,1,0:T(8,128)} %vert_hbm.1, s32[6,4]{1,0:T(8,128)} %copy.9.panel_ref, s32[6,4]{1,0:T(8,128)} %copy.10.side_ref, ...), custom_call_target="tpu_custom_call" | custom-call | tf_op jit(solution)/shard_map/pallas_call | solution.py:419
  26.8 0.0 copy-start
  26.8 1.7 %copy.14 = f32[6,6,12,16]{3,2,1,0:T(8,128)} copy(f32[6,6,12,16]{3,2,1,0:T(8,128)} %get-tuple-element.4) | data formatting | bytes 55296
  28.5 0.0 copy-done
  28.5 0.6 %copy.15 = f32[6,3,6,16]{3,2,1,0:T(8,128)} copy(f32[6,3,6,16]{3,2,1,0:T(8,128)S(1)} %copy-done) | data formatting | bytes 13824
Async XLA Ops:
  0.6 1.4 %copy-start.1 = (s32[6,4]{0,1:T(4,128)S(1)}, s32[6,4]{0,1:T(4,128)}, u32[]{:S(2)}) copy-start(s32[6,4]{0,1:T(4,128)} %param.12) | copy-start | bytes 292
  2.0 0.7 %copy-start.2 = (s32[6,4]{0,1:T(4,128)S(1)}, s32[6,4]{0,1:T(4,128)}, u32[]{:S(2)}) copy-start(s32[6,4]{0,1:T(4,128)} %param.13) | copy-start | bytes 292
  26.8 1.7 %copy-start = (f32[6,3,6,16]{3,2,1,0:T(8,128)S(1)}, f32[6,3,6,16]{3,2,1,0:T(8,128)}, u32[]{:S(2)}) copy-start(f32[6,3,6,16]{3,2,1,0:T(8,128)} %get-tuple-element.5) | copy-start | bytes 20740

commit v2 on v1

--- a/solution.py
+++ b/solution.py
@@ -145,8 +145,8 @@
         code = jnp.zeros_like(seg_lane)
         for p in range(panels):
             here = seg_lane // levels == p
-            index = jnp.where(here, panel_ref[p, side] * levels + seg_lane % levels, index)
-            code = jnp.where(here, flip_ref[p, side] * 4 + side_ref[p, side], code)
+            index = jnp.where(here, panel_ref[side, p] * levels + seg_lane % levels, index)
+            code = jnp.where(here, flip_ref[side, p] * 4 + side_ref[side, p], code)
         return index, code
 
     row_pick = pick_tables(tr)
@@ -442,7 +442,7 @@
                 pltpu.SemaphoreType.DMA((3, 8)),
             ],
             compiler_params=pltpu.CompilerParams(collective_id=0, has_side_effects=True),
-        )(residual, density, gain, vertical, edge_panel, edge_side, edge_flip)
+        )(residual, density, gain, vertical, edge_panel.T, edge_side.T, edge_flip.T)
 
     fields = P(None, "tx", "ty", None)
     return jax.shard_map(

time: 29.4 us -> 26.5 us (0.901)
  local copies, waits for them, and re-layouts: 5.09 us -> 2.36 us
    unnamed x11 -> x4, local copies, waits for them, and re-layouts: 5.09 us -> 2.36 us
where the time goes in v2:
time: 26.5 us; the launch traced here: 26.3 us
  Pallas kernels  23.3 us (88%)
  local copies, waits for them, and re-layouts  2.36 us (9%)
  between operations  0.65 us (2%)
    pallas_call x1, Pallas kernels, shards(): pl.pallas_call(functools.partial(kernel, nr, nc), out_shape=(jax.ShapeDty...  23.3 us
    unnamed x4, local copies, waits for them, and re-layouts  2.36 us

profile of v2, /device:TPU:0, one launch (start us, length us, event | category | flops | bytes accessed | tf_op | source)
XLA Modules:
  0.0 26.3 jit_solution(1345126498647203903)
XLA Ops:
  0.6 23.3 %shard_map.86 = (f32[6,6,12,16]{3,2,1,0:T(8,128)}, f32[6,3,6,16]{3,2,1,0:T(8,128)}) custom-call(f32[6,6,12,16]{3,2,1,0:T(8,128)} %res_hbm.1, f32[6,6,12,16]{3,2,1,0:T(8,128)} %den_hbm.1, f32[6,6,12,16]{3,2,1,0:T(8,128)} %gain_hbm.1, f32[6,6,12,16]{3,2,1,0:T(8,128)} %vert_hbm.1, s32[4,6]{1,0:T(4,128)} %bitcast.3, s32[4,6]{1,0:T(4,128)} %bitcast.4, s32[4,6]{1,0:T(4,128)} %bitcast.5), custom_call_target="tpu_custom_call" | custom-call | tf_op jit(solution)/shard_map/pallas_call | solution.py:419
  24.0 0.0 copy-start
  24.0 1.7 %copy.11 = f32[6,6,12,16]{3,2,1,0:T(8,128)} copy(f32[6,6,12,16]{3,2,1,0:T(8,128)} %get-tuple-element.4) | data formatting | bytes 55296
  25.7 0.0 copy-done
  25.7 0.6 %copy.12 = f32[6,3,6,16]{3,2,1,0:T(8,128)} copy(f32[6,3,6,16]{3,2,1,0:T(8,128)S(1)} %copy-done) | data formatting | bytes 13824
Async XLA Ops:
  24.0 1.7 %copy-start = (f32[6,3,6,16]{3,2,1,0:T(8,128)S(1)}, f32[6,3,6,16]{3,2,1,0:T(8,128)}, u32[]{:S(2)}) copy-start(f32[6,3,6,16]{3,2,1,0:T(8,128)} %get-tuple-element.5) | copy-start | bytes 20740

commit v3 on v2

--- a/solution.py
+++ b/solution.py
@@ -56,10 +56,6 @@
 
     def messages(n):
         found = []
-        found.append((r > 0, (r - 1, c), st_row.at[n, 0], nb_row.at[n, 1], nb_sem.at[n, 1]))
-        found.append((r < nr - 1, (r + 1, c), st_row.at[n, 1], nb_row.at[n, 0], nb_sem.at[n, 0]))
-        found.append((c > 0, (r, c - 1), st_col.at[n, 0], nb_col.at[n, 1], nb_sem.at[n, 3]))
-        found.append((c < nc - 1, (r, c + 1), st_col.at[n, 1], nb_col.at[n, 0], nb_sem.at[n, 2]))
         for i in range(k):
             src = st_row.at[n, tr, i]
             for f in range(2):
@@ -103,6 +99,10 @@
                 found.append(
                     (is_col, (g, e * (nc - 1)), src, rx_col.at[n, slot], col_sem.at[n, slot])
                 )
+        found.append((r > 0, (r - 1, c), st_row.at[n, 0], nb_row.at[n, 1], nb_sem.at[n, 1]))
+        found.append((r < nr - 1, (r + 1, c), st_row.at[n, 1], nb_row.at[n, 0], nb_sem.at[n, 0]))
+        found.append((c > 0, (r, c - 1), st_col.at[n, 0], nb_col.at[n, 1], nb_sem.at[n, 3]))
+        found.append((c < nc - 1, (r, c + 1), st_col.at[n, 1], nb_col.at[n, 0], nb_sem.at[n, 2]))
         return found
 
     def same(dest):
@@ -199,7 +199,7 @@
                     device_id_type=MESH,
                 ).start()
 
-            if m >= 4:
+            if m < 8 * k + 8:
 
                 @pl.when(active & mine)
                 def _():
@@ -429,10 +429,10 @@
                 pltpu.VMEM((4, panels, rows, cols, levels), f32),
                 pltpu.VMEM((3, rows, tall, LANES), f32),
                 pltpu.VMEM((rows, tall, LANES), f32),
-                pltpu.VMEM((3, 2, k, seg_h, LANES), f32),
-                pltpu.VMEM((3, 2, seg_h, LANES), f32),
-                pltpu.VMEM((3, 2, k, seg_h, LANES), f32),
-                pltpu.VMEM((3, 2, seg_h, LANES), f32),
+                pltpu.VMEM((4, 2, k, seg_h, LANES), f32),
+                pltpu.VMEM((4, 2, seg_h, LANES), f32),
+                pltpu.VMEM((4, 2, k, seg_h, LANES), f32),
+                pltpu.VMEM((4, 2, seg_h, LANES), f32),
                 pltpu.VMEM((3, 8, k, seg_h, LANES), f32),
                 pltpu.VMEM((3, 8, seg_h, LANES), f32),
                 pltpu.SemaphoreType.DMA((4,)),

time: 26.5 us -> 26.5 us (level)
  no operation moved by 1% of the time
where the time goes in v3:
time: 26.5 us; the launch traced here: 26.3 us
  Pallas kernels  23.3 us (88%)
  local copies, waits for them, and re-layouts  2.36 us (9%)
  between operations  0.65 us (2%)
    pallas_call x1, Pallas kernels, shards(): pl.pallas_call(functools.partial(kernel, nr, nc), out_shape=(jax.ShapeDty...  23.3 us
    unnamed x4, local copies, waits for them, and re-layouts  2.36 us

profile of v3, /device:TPU:0, one launch (start us, length us, event | category | flops | bytes accessed | tf_op | source)
XLA Modules:
  0.0 26.3 jit_solution(1710379868570947798)
XLA Ops:
  0.6 23.3 %shard_map.86 = (f32[6,6,12,16]{3,2,1,0:T(8,128)}, f32[6,3,6,16]{3,2,1,0:T(8,128)}) custom-call(f32[6,6,12,16]{3,2,1,0:T(8,128)} %res_hbm.1, f32[6,6,12,16]{3,2,1,0:T(8,128)} %den_hbm.1, f32[6,6,12,16]{3,2,1,0:T(8,128)} %gain_hbm.1, f32[6,6,12,16]{3,2,1,0:T(8,128)} %vert_hbm.1, s32[4,6]{1,0:T(4,128)} %bitcast.3, s32[4,6]{1,0:T(4,128)} %bitcast.4, s32[4,6]{1,0:T(4,128)} %bitcast.5), custom_call_target="tpu_custom_call" | custom-call | tf_op jit(solution)/shard_map/pallas_call | solution.py:419
  23.9 0.0 copy-start
  23.9 1.7 %copy.11 = f32[6,6,12,16]{3,2,1,0:T(8,128)} copy(f32[6,6,12,16]{3,2,1,0:T(8,128)} %get-tuple-element.4) | data formatting | bytes 55296
  25.6 0.0 copy-done
  25.6 0.6 %copy.12 = f32[6,3,6,16]{3,2,1,0:T(8,128)} copy(f32[6,3,6,16]{3,2,1,0:T(8,128)S(1)} %copy-done) | data formatting | bytes 13824
Async XLA Ops:
  23.9 1.7 %copy-start = (f32[6,3,6,16]{3,2,1,0:T(8,128)S(1)}, f32[6,3,6,16]{3,2,1,0:T(8,128)}, u32[]{:S(2)}) copy-start(f32[6,3,6,16]{3,2,1,0:T(8,128)} %get-tuple-element.5) | copy-start | bytes 20740

commit v4 on v3

--- a/solution.py
+++ b/solution.py
@@ -26,11 +26,10 @@
     panel_ref,
     side_ref,
     flip_ref,
-    sol_ref,
-    corr_ref,
+    spread,
+    small_ref,
     inp,
     packed,
-    spread,
     st_row,
     st_col,
     nb_row,
@@ -43,7 +42,7 @@
     row_sem,
     col_sem,
 ):
-    panels, rows, cols, levels = sol_ref.shape
+    _, panels, rows, cols, levels = inp.shape
     half_r, half_c = rows // 2, cols // 2
     k = cols // rows
     height = spread.shape[1] // 2
@@ -384,8 +383,7 @@
 
     bases = fine(base)
     for i in small:
-        for p in range(panels):
-            corr_ref[p, i] = correction[i][:half_c, p * levels : (p + 1) * levels]
+        small_ref[i] = correction[i]
     receive(2, half_r)
     left = [from_left(correction[i], nb_col[2, 0, i : i + 1, :]) for i in small]
     right = [from_right(correction[i], nb_col[2, 1, i : i + 1, :]) for i in small]
@@ -399,10 +397,17 @@
         if y == rows - 1:
             total = total + bottom
         spread[y, pl.ds(b, height, stride=2), :] = first + inverse[y][b] * total
-    for p in range(panels):
-        sol_ref[p] = spread[:, :cols, p * levels : (p + 1) * levels]
     for n in range(3):
         finish_sends(n)
+
+
+def unpack(spread, small_ref, sol_ref, corr_ref):
+    panels, _, cols, levels = sol_ref.shape
+    half_c = corr_ref.shape[2]
+    for p in range(panels):
+        lanes = slice(p * levels, (p + 1) * levels)
+        sol_ref[p] = spread[:, :cols, lanes]
+        corr_ref[p] = small_ref[:, :half_c, lanes]
 
 
 def solution(mesh):
@@ -416,11 +421,11 @@
         height = round_up(cols // 2, 8)
         tall = 2 * height
         f32 = jnp.float32
-        return pl.pallas_call(
+        spread, small = pl.pallas_call(
             functools.partial(kernel, nr, nc),
             out_shape=(
-                jax.ShapeDtypeStruct(residual.shape, f32),
-                jax.ShapeDtypeStruct((panels, rows // 2, cols // 2, levels), f32),
+                jax.ShapeDtypeStruct((rows, tall, LANES), f32),
+                jax.ShapeDtypeStruct((rows // 2, height, LANES), f32),
             ),
             in_specs=[pl.BlockSpec(memory_space=pl.ANY)] * 4
             + [pl.BlockSpec(memory_space=pltpu.SMEM)] * 3,
@@ -428,7 +433,6 @@
             scratch_shapes=[
                 pltpu.VMEM((4, panels, rows, cols, levels), f32),
                 pltpu.VMEM((3, rows, tall, LANES), f32),
-                pltpu.VMEM((rows, tall, LANES), f32),
                 pltpu.VMEM((4, 2, k, seg_h, LANES), f32),
                 pltpu.VMEM((4, 2, seg_h, LANES), f32),
                 pltpu.VMEM((4, 2, k, seg_h, LANES), f32),
@@ -443,6 +447,15 @@
             ],
             compiler_params=pltpu.CompilerParams(collective_id=0, has_side_effects=True),
         )(residual, density, gain, vertical, edge_panel.T, edge_side.T, edge_flip.T)
+        return pl.pallas_call(
+            unpack,
+            out_shape=(
+                jax.ShapeDtypeStruct(residual.shape, f32),
+                jax.ShapeDtypeStruct((panels, rows // 2, cols // 2, levels), f32),
+            ),
+            in_specs=[pl.BlockSpec(memory_space=pltpu.VMEM)] * 2,
+            out_specs=(pl.BlockSpec(memory_space=pltpu.VMEM),) * 2,
+        )(spread, small)
 
     fields = P(None, "tx", "ty", None)
     return jax.shard_map(

time: 26.5 us -> 25.6 us (0.966)
  local copies, waits for them, and re-layouts: 2.36 us -> 0 us
  Pallas kernels: 23.3 us -> 24.7 us
    unnamed x4 -> x0, local copies, waits for them, and re-layouts: 2.36 us -> none
    pallas_call x0 -> x1, Pallas kernels: none -> 1.67 us  [shards(): pl.pallas_call(unpack, out_shape=(jax.ShapeDtypeStruct(residual.shape, f3...]
where the time goes in v4:
time: 25.6 us; the launch traced here: 25.3 us
  Pallas kernels  24.7 us (96%)
  between operations  0.64 us (2%)
    pallas_call x1, Pallas kernels, shards(): pl.pallas_call(functools.partial(kernel, nr, nc), out_shape=(jax.ShapeDty...  23 us
    pallas_call x1, Pallas kernels, shards(): pl.pallas_call(unpack, out_shape=(jax.ShapeDtypeStruct(residual.shape, f3...  1.67 us

profile of v4, /device:TPU:0, one launch (start us, length us, event | category | flops | bytes accessed | tf_op | source)
XLA Modules:
  0.0 25.3 jit_solution(17043933451593448772)
XLA Ops:
  0.6 23.0 %shard_map.86 = (f32[6,16,128]{2,1,0:T(8,128)}, f32[3,8,128]{2,1,0:T(8,128)}) custom-call(f32[6,6,12,16]{3,2,1,0:T(8,128)} %res_hbm.1, f32[6,6,12,16]{3,2,1,0:T(8,128)} %den_hbm.1, f32[6,6,12,16]{3,2,1,0:T(8,128)} %gain_hbm.1, f32[6,6,12,16]{3,2,1,0:T(8,128)} %vert_hbm.1, s32[4,6]{1,0:T(4,128)} %bitcast.3, s32[4,6]{1,0:T(4,128)} %bitcast.4, s32[4,6]{1,0:T(4,128)} %bitcast.5), custom_call_target="tpu_custom_call" | custom-call | tf_op jit(solution)/shard_map/pallas_call | solution.py:424
  23.7 1.7 %shard_map.87 = (f32[6,6,12,16]{3,2,1,0:T(8,128)}, f32[6,3,6,16]{3,2,1,0:T(8,128)}) custom-call(f32[6,16,128]{2,1,0:T(8,128)} %get-tuple-element.4.spread, f32[3,8,128]{2,1,0:T(8,128)} %get-tuple-element.5.small_ref), custom_call_target="tpu_custom_call" | custom-call | tf_op jit(solution)/shard_map/pallas_call | solution.py:450
